TPU v7x, 256 devices: a whole 4x4x8 slice. The times are simulated.
256 devices in a mesh: tm: 8 (over x, y_hi), rows: 32 (over y_lo, z, core).
Axes of the slice: x: 4, y: 4 (y_hi: 2, y_lo: 2; y = y_hi * 2 + y_lo), z: 8, core: 2. Of those that a mesh axis runs over, the one named last changes fastest.
Arguments:
- frames_in: bfloat16 [32, 512, 64, 128], P('tm', 'rows'), may hold values from -6 to 6
- conv_one: bfloat16 [64, 3, 3, 64], replicated, may hold values from -0.375 to 0.375
- conv_two: bfloat16 [64, 3, 3, 64], replicated, may hold values from -0.375 to 0.375
- temporal: bfloat16 [3, 64, 64], replicated, may hold values from -0.625 to 0.625
- conv_three: bfloat16 [64, 3, 3, 64], replicated, may hold values from -0.375 to 0.375
- conv_four: bfloat16 [64, 3, 3, 64], replicated, may hold values from -0.375 to 0.375
- cotangent: bfloat16 [32, 512, 64, 128], P('tm', 'rows'), may hold values from -6 to 6
Outputs:
- decoded: bfloat16 [32, 512, 64, 128], P('tm', 'rows')
- grad_in: float32 [32, 512, 64, 128], P('tm', 'rows')
All inputs are finite; a program needn't handle non-finite values.
Results may differ from a plain program's by a relative error of at most 0.013.
Values may be sent and summed in bfloat16 or wider, within the bound.
A program may use at most 64 MiB of HBM per device.

v0:
```python
import functools

import jax
import jax.numpy as jnp
from jax import lax
from jax.experimental import pallas as pl
from jax.experimental.pallas import tpu as pltpu
from jax.sharding import PartitionSpec as P

SQRT_HALF = 0.7071067811865476
INV_ROOT_TAU = 0.3989422804014327
MESH = pl.DeviceIdType.MESH
C = 64
W = 128
PIECES = ((0, 2), (14, 16), (2, 8), (8, 14))


def gelu_both(v):
    phi = 0.5 + 0.5 * lax.erf(v * SQRT_HALF)
    bump = jnp.exp(v * v * -0.5) * INV_ROOT_TAU
    return v * phi, phi + v * bump


def kernel(sizes, x_hbm, k1, k2, t_hbm, k3, k4, cot_hbm, dec_hbm, grad_hbm,
           x1, xc, x3, x5, act1, sl1, act2, sl2, sl3, act4, bk4, b3, bk1, dec, grad, fw, bw, tf, tb, kraw, traw,
           w_sem, in_sem, out_sem, hs, hr, x3s, x3r, x5s, x5r, a_s, a_r, b_s, b_r):
    n_tm, n_rows, rows = sizes
    tm = lax.axis_index("tm")
    band = lax.axis_index("rows")
    has_up, has_down = band > 0, band < n_rows - 1
    has_prev, has_next = tm > 0, tm < n_tm - 1
    bf16, f32 = jnp.bfloat16, jnp.float32

    w_copies = [pltpu.make_async_copy(k, kraw.at[i], w_sem.at[i]) for i, k in enumerate((k1, k2, k3, k4))]
    w_copies.append(pltpu.make_async_copy(t_hbm, traw, w_sem.at[4]))
    for c in w_copies:
        c.start()

    def load(which, f):
        src, dst = ((x_hbm, x1), (cot_hbm, xc))[which]
        return pltpu.make_async_copy(
            src.at[f], dst.at[f // 2, 2:rows + 2, :, (f % 2) * W:(f % 2 + 1) * W], in_sem.at[which, f])

    for which, f in ((0, 2), (0, 3), (0, 0), (0, 1), (1, 2), (1, 3), (1, 0), (1, 1)):
        load(which, f).start()

    barrier = pltpu.get_barrier_semaphore()
    count = jnp.int32(0)
    for ok, peer in ((has_up, {"rows": band - 1}), (has_down, {"rows": band + 1}),
                     (has_prev, {"tm": tm - 1}), (has_next, {"tm": tm + 1})):
        @pl.when(ok)
        def _():
            pl.semaphore_signal(barrier, inc=1, device_id=peer, device_id_type=MESH)
        count = count + ok.astype(jnp.int32)
    pl.semaphore_wait(barrier, count)

    def border(src_of, dst_of, send, recv, at):
        down = pltpu.make_async_remote_copy(
            src_of(rows - 2), dst_of(0), send.at[*at, 0], recv.at[*at, 0],
            device_id={"rows": band + 1}, device_id_type=MESH)
        up = pltpu.make_async_remote_copy(
            src_of(0), dst_of(rows + 2), send.at[*at, 1], recv.at[*at, 1],
            device_id={"rows": band - 1}, device_id_type=MESH)
        return down, up

    def border_start(copies):
        down, up = copies

        @pl.when(has_down)
        def _():
            down.start()

        @pl.when(has_up)
        def _():
            up.start()

    def border_arrived(copies):
        down, up = copies

        @pl.when(has_up)
        def _():
            down.wait_recv()

        @pl.when(has_down)
        def _():
            up.wait_recv()

    def border_sent(copies):
        down, up = copies

        @pl.when(has_down)
        def _():
            down.wait_send()

        @pl.when(has_up)
        def _():
            up.wait_send()

    def input_border(which, f):
        src, dst = ((x_hbm, x1), (cot_hbm, xc))[which]
        half = slice((f % 2) * W, (f % 2 + 1) * W)
        return border(lambda r: src.at[f, r:r + 2], lambda r: dst.at[f // 2, r:r + 2, :, half], hs, hr, (which, f))

    def pair_border(buf, send, recv, p):
        return border(lambda r: buf.at[p, r + 2:r + 4], lambda r: buf.at[p, r:r + 2], send, recv, (p,))

    for which, f in ((0, 2), (0, 3), (0, 0), (0, 1), (1, 2), (1, 3), (1, 0), (1, 1)):
        border_start(input_border(which, f))

    def a_piece(i):
        lo, hi = PIECES[i]
        return pltpu.make_async_remote_copy(
            act2.at[2, lo:hi], act2.at[0, lo:hi], a_s.at[i], a_r.at[i], device_id={"tm": tm + 1}, device_id_type=MESH)

    def b_piece(i):
        lo, hi = PIECES[i]
        return pltpu.make_async_remote_copy(
            b3.at[0, lo:hi], b3.at[2, lo:hi], b_s.at[i], b_r.at[i], device_id={"tm": tm - 1}, device_id_type=MESH)

    def when_start(ok, copy):
        @pl.when(ok)
        def _():
            copy.start()

    def when_recv(ok, copy):
        @pl.when(ok)
        def _():
            copy.wait_recv()

    def when_sent(ok, copy):
        @pl.when(ok)
        def _():
            copy.wait_send()

    edge = jnp.zeros((2, C, 2 * W), bf16)

    @pl.when(jnp.logical_not(has_up))
    def _():
        for buf in (x1, xc, x3, x5):
            for p in range(2):
                buf[p, 0:2] = edge

    @pl.when(jnp.logical_not(has_down))
    def _():
        for buf in (x1, xc, x3, x5):
            for p in range(2):
                buf[p, rows + 2:rows + 4] = edge

    def clear(ref, at):
        def one(r, _):
            ref[at, r] = edge[0]
            return 0
        lax.fori_loop(0, rows, one, 0)

    @pl.when(jnp.logical_not(has_prev))
    def _():
        clear(act2, 0)

    @pl.when(jnp.logical_not(has_next))
    def _():
        clear(b3, 2)

    def arrange(n):
        w_copies[n].wait()
        for b in range(3):
            blocks = [kraw[n, a, b].astype(f32) for a in range(3)]
            fw[n, b * C:(b + 1) * C, :] = jnp.concatenate(blocks, axis=1).astype(bf16)
            bw[n, (2 - b) * C:(3 - b) * C, :] = jnp.concatenate([k.T for k in blocks[::-1]], axis=1).astype(bf16)

    for n in range(4):
        arrange(n)
    w_copies[4].wait()
    lags = [traw[j].astype(f32) for j in range(3)]
    tf[...] = jnp.concatenate(lags, axis=1).astype(bf16)
    tb[...] = jnp.concatenate([k.T for k in lags[::-1]], axis=1).astype(bf16)

    lane = lax.broadcasted_iota(jnp.int32, (C, W), 1)
    first_lane, last_lane = lane == 0, lane == W - 1

    def conv_row(src, p, weights, r):
        y = jnp.dot(weights, src[p, pl.ds(r, 3)].reshape(3 * C, 2 * W), preferred_element_type=f32)
        out = []
        for q in range(2):
            part = y[:, q * W:(q + 1) * W]
            left = jnp.where(first_lane, 0.0, pltpu.roll(part[0:C], 1, 1))
            right = jnp.where(last_lane, 0.0, pltpu.roll(part[2 * C:], W - 1, 1))
            out.append(left + part[C:2 * C] + right)
        return out

    halves = tuple(enumerate((slice(0, W), slice(W, 2 * W))))

    def loop(lo, hi, body):
        def one(r, _):
            body(r)
            return 0
        count = hi - lo
        step = next(u for u in (9, 8, 7, 6, 4, 3, 2, 1) if count % u == 0)
        lax.fori_loop(lo, hi, one, 0, unroll=step)

    def mid_one(p, lo, hi):
        def body(m):
            for (q, s), v in zip(halves, conv_row(x1, p, fw[0], m)):
                act, slope = gelu_both(v)
                act1[p, m, :, s] = act.astype(bf16)
                sl1[p, m, :, s] = slope.astype(bf16)
        loop(lo, hi, body)

    def second(p, lo, hi):
        def body(r):
            for (q, s), v in zip(halves, conv_row(act1, p, fw[1], r)):
                act, slope = gelu_both(v)
                act2[p + 1, r, :, s] = act.astype(bf16)
                sl2[p, r, :, s] = slope.astype(bf16)
        loop(lo, hi, body)

    def three(buf, first, r):
        early, late = buf[first, r], buf[first + 1, r]
        middle = jnp.concatenate([early[:, W:], late[:, :W]], axis=1)
        return early, middle, late

    def mix(p, lo, hi):
        def body(r):
            columns = jnp.concatenate(three(act2, p, r), axis=0)
            v = jnp.dot(tf[...], columns, preferred_element_type=f32)
            act, slope = gelu_both(v)
            x3[p, r + 2] = act.astype(bf16)
            sl3[p, r] = slope.astype(bf16)
        loop(lo, hi, body)

    def mid_four(p, lo, hi):
        def body(m):
            pre = conv_row(x3, p, fw[2], m)
            back = conv_row(xc, p, bw[3], m)
            for (q, s), v, g in zip(halves, pre, back):
                act, slope = gelu_both(v)
                act4[p, m, :, s] = act.astype(bf16)
                bk4[p, m, :, s] = (g * slope).astype(bf16)
        loop(lo, hi, body)

    def decode(p, lo, hi):
        def body(r):
            for (q, s), v in zip(halves, conv_row(act4, p, fw[3], r)):
                dec[p, r, :, s] = v.astype(bf16)
        loop(lo, hi, body)

    def back_three(p, lo, hi):
        def body(r):
            for (q, s), g in zip(halves, conv_row(bk4, p, bw[2], r)):
                b3[p, r, :, s] = (g * sl3[p, r, :, s].astype(f32)).astype(bf16)
        loop(lo, hi, body)

    def unmix(p, lo, hi):
        def body(r):
            columns = jnp.concatenate(three(b3, p, r), axis=0)
            g = jnp.dot(tb[...], columns, preferred_element_type=f32)
            x5[p, r + 2] = (g * sl2[p, r].astype(f32)).astype(bf16)
        loop(lo, hi, body)

    def back_one(p, lo, hi):
        def body(m):
            for (q, s), g in zip(halves, conv_row(x5, p, bw[1], m)):
                bk1[p, m, :, s] = (g * sl1[p, m, :, s].astype(f32)).astype(bf16)
        loop(lo, hi, body)

    def grads(p, lo, hi):
        def body(r):
            for (q, s), g in zip(halves, conv_row(bk1, p, bw[0], r)):
                grad[p, r, :, s] = g
        loop(lo, hi, body)

    def outside(p, bufs):
        @pl.when(jnp.logical_not(has_up))
        def _():
            for buf in bufs:
                buf[p, 0] = edge[0]

        @pl.when(jnp.logical_not(has_down))
        def _():
            for buf in bufs:
                buf[p, rows + 1] = edge[0]

    def store(which, f):
        src, dst = ((dec, dec_hbm), (grad, grad_hbm))[which]
        return pltpu.make_async_copy(
            src.at[f // 2, :, :, (f % 2) * W:(f % 2 + 1) * W], dst.at[f], out_sem.at[which, f])

    def stage_one(p):
        for f in (2 * p, 2 * p + 1):
            load(0, f).wait()
        mid_one(p, 2, rows)
        for f in (2 * p, 2 * p + 1):
            border_arrived(input_border(0, f))
        mid_one(p, 0, 2)
        mid_one(p, rows, rows + 2)
        outside(p, (act1, sl1))

    def start_pair(p):
        mid_four(p, 2, rows)
        border_arrived(pair_border(x3, x3s, x3r, p))
        mid_four(p, 0, 2)
        mid_four(p, rows, rows + 2)
        outside(p, (act4, bk4))

    stage_one(1)
    for i, (lo, hi) in enumerate(PIECES):
        second(1, lo, hi)
        when_start(has_next, a_piece(i))
    stage_one(0)
    second(0, 0, rows)
    for lo, hi in PIECES[:2]:
        mix(1, lo, hi)
    border_start(pair_border(x3, x3s, x3r, 1))
    mix(1, 2, rows - 2)
    for f in (2, 3):
        load(1, f).wait()
        border_arrived(input_border(1, f))
    start_pair(1)
    back_three(1, 0, rows)
    decode(1, 0, rows)
    for f in (2, 3):
        store(0, f).start()
    for f in (0, 1):
        load(1, f).wait()
        border_arrived(input_border(1, f))

    for i in (0, 1):
        when_recv(has_prev, a_piece(i))
        mix(0, *PIECES[i])
    border_start(pair_border(x3, x3s, x3r, 0))
    for i in (2, 3):
        when_recv(has_prev, a_piece(i))
        mix(0, *PIECES[i])
    start_pair(0)
    for i, (lo, hi) in enumerate(PIECES):
        back_three(0, lo, hi)
        when_start(has_prev, b_piece(i))
    for lo, hi in PIECES[:2]:
        unmix(0, lo, hi)
    border_start(pair_border(x5, x5s, x5r, 0))
    unmix(0, 2, rows - 2)
    decode(0, 0, rows)
    for f in (0, 1):
        store(0, f).start()
    border_arrived(pair_border(x5, x5s, x5r, 0))
    back_one(0, 0, rows + 2)
    grads(0, 0, rows)
    for f in (0, 1):
        store(1, f).start()

    for i in (0, 1):
        when_recv(has_next, b_piece(i))
        unmix(1, *PIECES[i])
    border_start(pair_border(x5, x5s, x5r, 1))
    for i in (2, 3):
        when_recv(has_next, b_piece(i))
        unmix(1, *PIECES[i])
    back_one(1, 2, rows)
    border_arrived(pair_border(x5, x5s, x5r, 1))
    back_one(1, 0, 2)
    back_one(1, rows, rows + 2)
    grads(1, 0, rows)
    for f in (2, 3):
        store(1, f).start()

    for which in range(2):
        for f in range(4):
            border_sent(input_border(which, f))
    for p in range(2):
        border_sent(pair_border(x3, x3s, x3r, p))
        border_sent(pair_border(x5, x5s, x5r, p))
    for i in range(len(PIECES)):
        when_sent(has_next, a_piece(i))
        when_sent(has_prev, b_piece(i))
    for which in range(2):
        for f in range(4):
            store(which, f).wait()


def per_device(sizes, frames_in, conv_one, conv_two, temporal, conv_three, conv_four, cotangent):
    frames, rows = frames_in.shape[:2]
    sizes = (*sizes, rows)
    taps = [jnp.transpose(k, (1, 2, 0, 3)) for k in (conv_one, conv_two, conv_three, conv_four)]
    bf16, f32 = jnp.bfloat16, jnp.float32

    def pair(extra, kind=bf16, count=2):
        return pltpu.VMEM((count, rows + extra, C, 2 * W), kind)

    dma = pltpu.SemaphoreType.DMA
    hbm = pl.BlockSpec(memory_space=pl.ANY)
    return pl.pallas_call(
        functools.partial(kernel, sizes),
        name="stack",
        out_shape=(jax.ShapeDtypeStruct(frames_in.shape, bf16), jax.ShapeDtypeStruct(frames_in.shape, f32)),
        in_specs=[hbm] * 7,
        out_specs=(hbm, hbm),
        scratch_shapes=[
            pair(4), pair(4), pair(4), pair(4),
            pair(2), pair(2),
            pair(0, count=3), pair(0), pair(0),
            pair(2), pair(2),
            pair(0, count=3),
            pair(2),
            pair(0), pair(0, f32),
            pltpu.VMEM((4, 3 * C, 3 * C), bf16), pltpu.VMEM((4, 3 * C, 3 * C), bf16),
            pltpu.VMEM((C, 3 * C), bf16), pltpu.VMEM((C, 3 * C), bf16),
            pltpu.VMEM((4, 3, 3, C, C), bf16), pltpu.VMEM((3, C, C), bf16),
            dma((5,)), dma((2, 4)), dma((2, 4)),
            dma((2, 4, 2)), dma((2, 4, 2)),
            dma((2, 2)), dma((2, 2)), dma((2, 2)), dma((2, 2)),
            dma((4,)), dma((4,)), dma((4,)), dma((4,)),
        ],
        compiler_params=pltpu.CompilerParams(collective_id=0, has_side_effects=True, vmem_limit_bytes=56 << 20),
    )(frames_in, taps[0], taps[1], temporal, taps[2], taps[3], cotangent)


def solution(mesh):
    split = P("tm", "rows", None, None)
    return jax.shard_map(
        functools.partial(per_device, (mesh.shape["tm"], mesh.shape["rows"])),
        mesh=mesh,
        in_specs=(split, P(), P(), P(), P(), P(), split),
        out_specs=(split, split),
        check_vma=False,
    )
```

profile of v0, /device:TPU:1, one launch (start us, length us, event | category | flops | bytes accessed | tf_op | source)
XLA Modules:
  0.0 51.4 jit_solution(17700564610365620673)
XLA Ops:
  0.6 47.0 %stack.1 = (bf16[4,16,64,128]{3,2,1,0:T(8,128)(2,1)}, f32[4,16,64,128]{3,2,1,0:T(8,128)}) custom-call(bf16[4,16,64,128]{3,2,1,0:T(8,128)(2,1)} %x_hbm.1, bf16[3,3,64,64]{3,2,1,0:T(8,128)(2,1)} %bitcast.4, bf16[3,3,64,64]{3,2,1,0:T(8,128)(2,1)} %bitcast.5, bf16[3,64,64]{2,1,0:T(8,128)(2,1)} %t_hbm.1, bf16[3,3,64,64]{3,2,1,0:T(8,128)(2,1)} %bitcast.6, ...), custom_call_target="tpu_custom_call" | custom-call | tf_op jit(solution)/shard_map/stack/pallas_call | solution.py:390
  47.6 0.0 copy-start
  47.6 2.4 %copy.11 = bf16[4,16,64,128]{3,2,1,0:T(8,128)(2,1)} copy(bf16[4,16,64,128]{3,2,1,0:T(8,128)(2,1)} %get-tuple-element.4) | data formatting | bytes 2097152
  50.0 0.0 copy-done
  50.0 1.3 %copy.12 = f32[4,16,64,128]{3,2,1,0:T(8,128)} copy(f32[4,16,64,128]{3,2,1,0:T(8,128)S(1)} %copy-done) | data formatting | bytes 4194304
Async XLA Ops:
  47.6 2.4 %copy-start = (f32[4,16,64,128]{3,2,1,0:T(8,128)S(1)}, f32[4,16,64,128]{3,2,1,0:T(8,128)}, u32[]{:S(2)}) copy-start(f32[4,16,64,128]{3,2,1,0:T(8,128)} %get-tuple-element.5) | copy-start | bytes 6291460
where the time goes:
time: 51.4 us
  Pallas kernels  47 us (91%)
  local copies, waits for them, and re-layouts  3.73 us (7%)
  between operations  0.65 us (1%)
    pallas_call x1, Pallas kernels, per_device(): pl.pallas_call(functools.partial(kernel, sizes), name='stack', out_shape=...  47 us
    unnamed x4, local copies, waits for them, and re-layouts  3.73 us

commit v1 on v0

v1 whole, which is shorter than its diff:
```python
import functools

import jax
import jax.numpy as jnp
from jax import lax
from jax.experimental import pallas as pl
from jax.experimental.pallas import tpu as pltpu
from jax.sharding import PartitionSpec as P

SQRT_HALF = 0.7071067811865476
INV_ROOT_TAU = 0.3989422804014327
MESH = pl.DeviceIdType.MESH
C = 64
W = 128
PIECES = ((0, 2), (14, 16), (2, 8), (8, 14))
BACK_PIECES = ((0, 6), (14, 16), (6, 10), (10, 14))


def gelu_both(v):
    phi = 0.5 + 0.5 * lax.erf(v * SQRT_HALF)
    bump = jnp.exp(v * v * -0.5) * INV_ROOT_TAU
    return v * phi, phi + v * bump


def conv_row(window, weights):
    lane = lax.broadcasted_iota(jnp.int32, (C, W), 1)
    y = jnp.dot(weights, window.reshape(3 * C, 2 * W), preferred_element_type=jnp.float32)
    out = []
    for q in range(2):
        part = y[:, q * W:(q + 1) * W]
        left = jnp.where(lane == 0, 0.0, pltpu.roll(part[0:C], 1, 1))
        right = jnp.where(lane == W - 1, 0.0, pltpu.roll(part[2 * C:], W - 1, 1))
        out.append(left + part[C:2 * C] + right)
    return out


HALVES = (slice(0, W), slice(W, 2 * W))


def loop(lo, hi, body):
    def one(r, _):
        body(r)
        return 0
    lax.fori_loop(lo, hi, one, 0, unroll=hi - lo)


def last_kernel(rows, dec, grad0, bk1, bw1, dec_hbm, grad_hbm, grad1, sem):
    def store(which, f):
        src, dst = ((dec.at[f // 2], dec_hbm), ((grad0, grad1)[f // 2], grad_hbm))[which]
        return pltpu.make_async_copy(src.at[:, :, HALVES[f % 2]], dst.at[f], sem.at[which, f])

    for which, f in ((0, 0), (0, 1), (0, 2), (0, 3), (1, 0), (1, 1)):
        store(which, f).start()

    def body(r):
        for s, g in zip(HALVES, conv_row(bk1[pl.ds(r, 3)], bw1[...])):
            grad1[r, :, s] = g
    loop(0, rows, body)
    for f in (2, 3):
        store(1, f).start()
    for which in range(2):
        for f in range(4):
            store(which, f).wait()


def kernel(sizes, x_hbm, k1, k2, t_hbm, k3, k4, cot_hbm, dec, grad0, bk1_late, bw1,
           x1, xc, x3, x5, act1, sl1, act2, sl2, sl3, act4, bk4, b3, bk1_early, fw, bw, tf, tb, kraw, traw,
           w_sem, in_sem, hs, hr, x3s, x3r, x5s, x5r, a_s, a_r, b_s, b_r):
    n_tm, n_rows, rows = sizes
    tm = lax.axis_index("tm")
    band = lax.axis_index("rows")
    has_up, has_down = band > 0, band < n_rows - 1
    has_prev, has_next = tm > 0, tm < n_tm - 1
    bf16, f32 = jnp.bfloat16, jnp.float32

    w_copies = [pltpu.make_async_copy(k, kraw.at[i], w_sem.at[i]) for i, k in enumerate((k1, k2, k3, k4))]
    w_copies.append(pltpu.make_async_copy(t_hbm, traw, w_sem.at[4]))
    for c in w_copies:
        c.start()

    def load(which, f):
        src, dst = ((x_hbm, x1), (cot_hbm, xc))[which]
        return pltpu.make_async_copy(
            src.at[f], dst.at[f // 2, 2:rows + 2, :, (f % 2) * W:(f % 2 + 1) * W], in_sem.at[which, f])

    for which, f in ((0, 2), (0, 3), (0, 0), (0, 1), (1, 2), (1, 3), (1, 0), (1, 1)):
        load(which, f).start()

    barrier = pltpu.get_barrier_semaphore()
    count = jnp.int32(0)
    for ok, peer in ((has_up, {"rows": band - 1}), (has_down, {"rows": band + 1}),
                     (has_prev, {"tm": tm - 1}), (has_next, {"tm": tm + 1})):
        @pl.when(ok)
        def _():
            pl.semaphore_signal(barrier, inc=1, device_id=peer, device_id_type=MESH)
        count = count + ok.astype(jnp.int32)
    pl.semaphore_wait(barrier, count)

    def border(src_of, dst_of, send, recv, at):
        down = pltpu.make_async_remote_copy(
            src_of(rows - 2), dst_of(0), send.at[*at, 0], recv.at[*at, 0],
            device_id={"rows": band + 1}, device_id_type=MESH)
        up = pltpu.make_async_remote_copy(
            src_of(0), dst_of(rows + 2), send.at[*at, 1], recv.at[*at, 1],
            device_id={"rows": band - 1}, device_id_type=MESH)
        return down, up

    def border_start(copies):
        down, up = copies

        @pl.when(has_down)
        def _():
            down.start()

        @pl.when(has_up)
        def _():
            up.start()

    def border_arrived(copies):
        down, up = copies

        @pl.when(has_up)
        def _():
            down.wait_recv()

        @pl.when(has_down)
        def _():
            up.wait_recv()

    def border_sent(copies):
        down, up = copies

        @pl.when(has_down)
        def _():
            down.wait_send()

        @pl.when(has_up)
        def _():
            up.wait_send()

    def input_border(which, f):
        src, dst = ((x_hbm, x1), (cot_hbm, xc))[which]
        half = slice((f % 2) * W, (f % 2 + 1) * W)
        return border(lambda r: src.at[f, r:r + 2], lambda r: dst.at[f // 2, r:r + 2, :, half], hs, hr, (which, f))

    def pair_border(buf, send, recv, p):
        return border(lambda r: buf.at[p, r + 2:r + 4], lambda r: buf.at[p, r:r + 2], send, recv, (p,))

    for which, f in ((0, 2), (0, 3), (0, 0), (0, 1), (1, 2), (1, 3), (1, 0), (1, 1)):
        border_start(input_border(which, f))

    def a_piece(i):
        lo, hi = PIECES[i]
        return pltpu.make_async_remote_copy(
            act2.at[2, lo:hi], act2.at[0, lo:hi], a_s.at[i], a_r.at[i], device_id={"tm": tm + 1}, device_id_type=MESH)

    def b_piece(i):
        lo, hi = BACK_PIECES[i]
        return pltpu.make_async_remote_copy(
            b3.at[0, lo:hi], b3.at[2, lo:hi], b_s.at[i], b_r.at[i], device_id={"tm": tm - 1}, device_id_type=MESH)

    def when_start(ok, copy):
        @pl.when(ok)
        def _():
            copy.start()

    def when_recv(ok, copy):
        @pl.when(ok)
        def _():
            copy.wait_recv()

    def when_sent(ok, copy):
        @pl.when(ok)
        def _():
            copy.wait_send()

    edge = jnp.zeros((2, C, 2 * W), bf16)

    def clear_rows(bufs):
        @pl.when(jnp.logical_not(has_up))
        def _():
            for buf in bufs:
                for p in range(2):
                    buf[p, 0:2] = edge

        @pl.when(jnp.logical_not(has_down))
        def _():
            for buf in bufs:
                for p in range(2):
                    buf[p, rows + 2:rows + 4] = edge

    def clear(ref, at):
        def one(r, _):
            ref[at, r] = edge[0]
            return 0
        lax.fori_loop(0, rows, one, 0)

    def clear_frames():
        @pl.when(jnp.logical_not(has_prev))
        def _():
            clear(act2, 0)

        @pl.when(jnp.logical_not(has_next))
        def _():
            clear(b3, 2)

    def arrange(n):
        for b in range(3):
            fw[n, b * C:(b + 1) * C, :] = jnp.concatenate(
                [kraw[n, a, b].astype(f32) for a in range(3)], axis=1).astype(bf16)

    def arrange_back(n):
        ref = bw1 if n == 0 else bw.at[n - 1]
        for b in range(3):
            ref[b * C:(b + 1) * C, :] = jnp.concatenate(
                [kraw[n, 2 - a, 2 - b].astype(f32).T for a in range(3)], axis=1).astype(bf16)

    def arrange_lags():
        lags = [traw[j].astype(f32) for j in range(3)]
        tf[...] = jnp.concatenate(lags, axis=1).astype(bf16)
        tb[...] = jnp.concatenate([k.T for k in lags[::-1]], axis=1).astype(bf16)

    def mid_one(p, lo, hi):
        def body(m):
            for s, v in zip(HALVES, conv_row(x1[p, pl.ds(m, 3)], fw[0])):
                act, slope = gelu_both(v)
                act1[p, m, :, s] = act.astype(bf16)
                sl1[p, m, :, s] = slope.astype(bf16)
        loop(lo, hi, body)

    def second(p, lo, hi):
        def body(r):
            for s, v in zip(HALVES, conv_row(act1[p, pl.ds(r, 3)], fw[1])):
                act, slope = gelu_both(v)
                act2[p + 1, r, :, s] = act.astype(bf16)
                sl2[p, r, :, s] = slope.astype(bf16)
        loop(lo, hi, body)

    def three(buf, first, r):
        early, late = buf[first, r], buf[first + 1, r]
        middle = jnp.concatenate([early[:, W:], late[:, :W]], axis=1)
        return early, middle, late

    def mix(p, lo, hi):
        def body(r):
            columns = jnp.concatenate(three(act2, p, r), axis=0)
            v = jnp.dot(tf[...], columns, preferred_element_type=f32)
            act, slope = gelu_both(v)
            x3[p, r + 2] = act.astype(bf16)
            sl3[p, r] = slope.astype(bf16)
        loop(lo, hi, body)

    def mid_four(p, lo, hi):
        def body(m):
            pre = conv_row(x3[p, pl.ds(m, 3)], fw[2])
            back = conv_row(xc[p, pl.ds(m, 3)], bw[2])
            for s, v, g in zip(HALVES, pre, back):
                act, slope = gelu_both(v)
                act4[p, m, :, s] = act.astype(bf16)
                bk4[p, m, :, s] = (g * slope).astype(bf16)
        loop(lo, hi, body)

    def decode(p, lo, hi):
        def body(r):
            for s, v in zip(HALVES, conv_row(act4[p, pl.ds(r, 3)], fw[3])):
                dec[p, r, :, s] = v.astype(bf16)
        loop(lo, hi, body)

    def back_three(p, lo, hi):
        def body(r):
            for s, g in zip(HALVES, conv_row(bk4[p, pl.ds(r, 3)], bw[1])):
                b3[p, r, :, s] = (g * sl3[p, r, :, s].astype(f32)).astype(bf16)
        loop(lo, hi, body)

    def unmix(p, lo, hi):
        def body(r):
            columns = jnp.concatenate(three(b3, p, r), axis=0)
            g = jnp.dot(tb[...], columns, preferred_element_type=f32)
            x5[p, r + 2] = (g * sl2[p, r].astype(f32)).astype(bf16)
        loop(lo, hi, body)

    def back_one(p, lo, hi):
        bk1 = (bk1_early, bk1_late)[p]

        def body(m):
            for s, g in zip(HALVES, conv_row(x5[p, pl.ds(m, 3)], bw[0])):
                bk1[m, :, s] = (g * sl1[p, m, :, s].astype(f32)).astype(bf16)
        loop(lo, hi, body)

    def grads(lo, hi):
        def body(r):
            for s, g in zip(HALVES, conv_row(bk1_early[pl.ds(r, 3)], bw1[...])):
                grad0[r, :, s] = g
        loop(lo, hi, body)

    def outside_first(p, bufs):
        @pl.when(jnp.logical_not(has_up))
        def _():
            for buf in bufs:
                buf[p, 0] = edge[0]

    def outside_last(p, bufs):
        @pl.when(jnp.logical_not(has_down))
        def _():
            for buf in bufs:
                buf[p, rows + 1] = edge[0]

    def outside(p, bufs):
        outside_first(p, bufs)
        outside_last(p, bufs)

    def stage_one(p):
        for f in (2 * p, 2 * p + 1):
            load(0, f).wait()
        mid_one(p, 2, rows)
        for f in (2 * p, 2 * p + 1):
            border_arrived(input_border(0, f))
        mid_one(p, 0, 2)
        mid_one(p, rows, rows + 2)
        outside(p, (act1, sl1))

    w_copies[0].wait()
    arrange(0)
    clear_rows((x1,))
    stage_one(1)
    w_copies[1].wait()
    arrange(1)
    for i, (lo, hi) in enumerate(PIECES):
        second(1, lo, hi)
        when_start(has_next, a_piece(i))
    stage_one(0)
    second(0, 0, rows)
    clear_rows((xc, x3, x5))
    for i in (2, 3, 4):
        w_copies[i].wait()
    arrange_lags()
    for lo, hi in PIECES[:2]:
        mix(1, lo, hi)
    border_start(pair_border(x3, x3s, x3r, 1))
    mix(1, 2, rows - 2)
    arrange(2)
    arrange_back(3)
    for f in (2, 3):
        load(1, f).wait()
        border_arrived(input_border(1, f))
    mid_four(1, 2, rows)
    border_arrived(pair_border(x3, x3s, x3r, 1))
    mid_four(1, 0, 2)
    mid_four(1, rows, rows + 2)
    outside(1, (act4, bk4))
    arrange_back(2)
    back_three(1, 0, rows)
    arrange(3)
    decode(1, 0, rows)
    arrange_back(1)
    arrange_back(0)
    clear_frames()
    for f in (0, 1):
        load(1, f).wait()
        border_arrived(input_border(1, f))

    for i in (0, 1):
        when_recv(has_prev, a_piece(i))
        mix(0, *PIECES[i])
    border_start(pair_border(x3, x3s, x3r, 0))
    when_recv(has_prev, a_piece(2))
    mix(0, *PIECES[2])
    border_arrived(pair_border(x3, x3s, x3r, 0))
    mid_four(0, 0, 8)
    outside_first(0, (act4, bk4))
    back_three(0, *BACK_PIECES[0])
    when_start(has_prev, b_piece(0))
    when_recv(has_prev, a_piece(3))
    mix(0, *PIECES[3])
    mid_four(0, 8, rows + 2)
    outside_last(0, (act4, bk4))
    for i in (1, 2, 3):
        back_three(0, *BACK_PIECES[i])
        when_start(has_prev, b_piece(i))
    unmix(0, 0, 2)
    unmix(0, rows - 2, rows)
    border_start(pair_border(x5, x5s, x5r, 0))
    unmix(0, 2, rows - 2)
    decode(0, 0, rows)
    border_arrived(pair_border(x5, x5s, x5r, 0))
    back_one(0, 0, rows + 2)
    grads(0, rows)

    for i in (0, 1):
        when_recv(has_next, b_piece(i))
        unmix(1, *BACK_PIECES[i])
    border_start(pair_border(x5, x5s, x5r, 1))
    when_recv(has_next, b_piece(2))
    unmix(1, *BACK_PIECES[2])
    border_arrived(pair_border(x5, x5s, x5r, 1))
    back_one(1, 0, 10)
    when_recv(has_next, b_piece(3))
    unmix(1, *BACK_PIECES[3])
    back_one(1, 10, rows + 2)

    for which in range(2):
        for f in range(4):
            border_sent(input_border(which, f))
    for p in range(2):
        border_sent(pair_border(x3, x3s, x3r, p))
        border_sent(pair_border(x5, x5s, x5r, p))
    for i in range(len(PIECES)):
        when_sent(has_next, a_piece(i))
        when_sent(has_prev, b_piece(i))


def per_device(sizes, frames_in, conv_one, conv_two, temporal, conv_three, conv_four, cotangent):
    frames, rows = frames_in.shape[:2]
    sizes = (*sizes, rows)
    taps = [jnp.transpose(k, (1, 2, 0, 3)) for k in (conv_one, conv_two, conv_three, conv_four)]
    bf16, f32 = jnp.bfloat16, jnp.float32

    def pair(extra, count=2):
        return pltpu.VMEM((count, rows + extra, C, 2 * W), bf16)

    dma = pltpu.SemaphoreType.DMA
    hbm, vmem = pl.BlockSpec(memory_space=pltpu.HBM), pl.BlockSpec(memory_space=pltpu.VMEM)
    matrix = (3 * C, 3 * C)
    halfway = pl.pallas_call(
        functools.partial(kernel, sizes),
        name="stack",
        out_shape=(
            jax.ShapeDtypeStruct((2, rows, C, 2 * W), bf16),
            jax.ShapeDtypeStruct((rows, C, 2 * W), f32),
            jax.ShapeDtypeStruct((rows + 2, C, 2 * W), bf16),
            jax.ShapeDtypeStruct(matrix, bf16),
        ),
        in_specs=[hbm] * 7,
        out_specs=(vmem,) * 4,
        scratch_shapes=[
            pair(4), pair(4), pair(4), pair(4),
            pair(2), pair(2),
            pair(0, count=3), pair(0), pair(0),
            pair(2), pair(2),
            pair(0, count=3),
            pltpu.VMEM((rows + 2, C, 2 * W), bf16),
            pltpu.VMEM((4, *matrix), bf16), pltpu.VMEM((3, *matrix), bf16),
            pltpu.VMEM((C, 3 * C), bf16), pltpu.VMEM((C, 3 * C), bf16),
            pltpu.VMEM((4, 3, 3, C, C), bf16), pltpu.VMEM((3, C, C), bf16),
            dma((5,)), dma((2, 4)),
            dma((2, 4, 2)), dma((2, 4, 2)),
            dma((2, 2)), dma((2, 2)), dma((2, 2)), dma((2, 2)),
            dma((4,)), dma((4,)), dma((4,)), dma((4,)),
        ],
        compiler_params=pltpu.CompilerParams(collective_id=0, has_side_effects=True, vmem_limit_bytes=36 << 20),
    )(*[pltpu.with_memory_space_constraint(v, pltpu.HBM) for v in (frames_in, taps[0], taps[1], temporal, taps[2], taps[3], cotangent)])
    return pl.pallas_call(
        functools.partial(last_kernel, rows),
        name="last",
        out_shape=(jax.ShapeDtypeStruct(frames_in.shape, bf16), jax.ShapeDtypeStruct(frames_in.shape, f32)),
        in_specs=[vmem] * 4,
        out_specs=(hbm, hbm),
        scratch_shapes=[pltpu.VMEM((rows, C, 2 * W), f32), dma((2, 4))],
        compiler_params=pltpu.CompilerParams(vmem_limit_bytes=16 << 20),
    )(*halfway)


def solution(mesh):
    split = P("tm", "rows", None, None)
    return jax.shard_map(
        functools.partial(per_device, (mesh.shape["tm"], mesh.shape["rows"])),
        mesh=mesh,
        in_specs=(split, P(), P(), P(), P(), P(), split),
        out_specs=(split, split),
        check_vma=False,
    )
```

time: 51.4 us -> 45.8 us (0.89)
  the two profiles are of different devices: /device:TPU:1 before, /device:TPU:10 now
where the time goes in v1:
time: 45.8 us; the launch traced here: 45.7 us
  Pallas kernels  44.9 us (98%)
  between operations  0.8 us (2%)
    pallas_call x1, Pallas kernels, per_device(): pl.pallas_call(functools.partial(kernel, sizes), name='stack', out_shape=...  42.7 us
    pallas_call x1, Pallas kernels, per_device(): pl.pallas_call(functools.partial(last_kernel, rows), name='last', out_sha...  2.2 us

profile of v1, /device:TPU:10, one launch (start us, length us, event | category | flops | bytes accessed | tf_op | source)
XLA Modules:
  0.0 45.7 jit_solution(15337025937286355360)
XLA Ops:
  0.6 42.7 %stack.1 = (bf16[2,16,64,256]{3,2,1,0:T(8,128)(2,1)S(1)}, f32[16,64,256]{2,1,0:T(8,128)S(1)}, bf16[18,64,256]{2,1,0:T(8,128)(2,1)S(1)}, bf16[192,192]{1,0:T(8,128)(2,1)S(1)}) custom-call(bf16[4,16,64,128]{3,2,1,0:T(8,128)(2,1)} %x_hbm.1, bf16[3,3,64,64]{3,2,1,0:T(8,128)(2,1)} %bitcast.4, bf16[3,3,64,64]{3,2,1,0:T(8,128)(2,1)} %bitcast.5, ...), custom_call_target="tpu_custom_call" | custom-call | tf_op jit(solution)/shard_map/stack/pallas_call | solution.py:424
  43.3 2.2 %last.1 = (bf16[4,16,64,128]{3,2,1,0:T(8,128)(2,1)}, f32[4,16,64,128]{3,2,1,0:T(8,128)}) custom-call(bf16[2,16,64,256]{3,2,1,0:T(8,128)(2,1)S(1)} %get-tuple-element.6.dec, f32[16,64,256]{2,1,0:T(8,128)S(1)} %get-tuple-element.7.grad0, bf16[18,64,256]{2,1,0:T(8,128)(2,1)S(1)} %get-tuple-element.8.bk1, bf16[192,192]{1,0:T(8,128)(2,1)S(1)} %get-tuple-element.9.bw1), custom_call_target="tpu_custom_call" | custom-call | tf_op jit(solution)/shard_map/last/pallas_call | solution.py:452

commit v2 on v1

--- a/solution.py
+++ b/solution.py
@@ -12,8 +12,8 @@
 MESH = pl.DeviceIdType.MESH
 C = 64
 W = 128
-PIECES = ((0, 2), (14, 16), (2, 8), (8, 14))
-BACK_PIECES = ((0, 6), (14, 16), (6, 10), (10, 14))
+PIECES = ((2, 6), (0, 2), (14, 16), (6, 10), (10, 14))
+BACK_PIECES = ((0, 4), (4, 8), (14, 16), (8, 11), (11, 14))
 
 
 def gelu_both(v):
@@ -64,7 +64,7 @@
 
 
 def kernel(sizes, x_hbm, k1, k2, t_hbm, k3, k4, cot_hbm, dec, grad0, bk1_late, bw1,
-           x1, xc, x3, x5, act1, sl1, act2, sl2, sl3, act4, bk4, b3, bk1_early, fw, bw, tf, tb, kraw, traw,
+           x1, xc, x3, x5, act1, sl1, act2, sl2, sl3, act4, bk4, g4, b3, bk1_early, fw, bw, tf, tb, kraw, traw,
            w_sem, in_sem, hs, hr, x3s, x3r, x5s, x5r, a_s, a_r, b_s, b_r):
     n_tm, n_rows, rows = sizes
     tm = lax.axis_index("tm")
@@ -253,13 +253,19 @@
     def mid_four(p, lo, hi):
         def body(m):
             pre = conv_row(x3[p, pl.ds(m, 3)], fw[2])
-            back = conv_row(xc[p, pl.ds(m, 3)], bw[2])
+            back = conv_row(xc[p, pl.ds(m, 3)], bw[2]) if p else [g4[m, :, s] for s in HALVES]
             for s, v, g in zip(HALVES, pre, back):
                 act, slope = gelu_both(v)
                 act4[p, m, :, s] = act.astype(bf16)
                 bk4[p, m, :, s] = (g * slope).astype(bf16)
         loop(lo, hi, body)
 
+    def back_cotangent(lo, hi):
+        def body(m):
+            for s, g in zip(HALVES, conv_row(xc[0, pl.ds(m, 3)], bw[2])):
+                g4[m, :, s] = g
+        loop(lo, hi, body)
+
     def decode(p, lo, hi):
         def body(r):
             for s, v in zip(HALVES, conv_row(act4[p, pl.ds(r, 3)], fw[3])):
@@ -309,94 +315,110 @@
         outside_first(p, bufs)
         outside_last(p, bufs)
 
-    def stage_one(p):
+    def edges(step, p, extra=0):
+        step(p, 0, 2)
+        step(p, rows - 2 + extra, rows + extra)
+
+    def input_arrived(which, p):
         for f in (2 * p, 2 * p + 1):
-            load(0, f).wait()
-        mid_one(p, 2, rows)
-        for f in (2 * p, 2 * p + 1):
-            border_arrived(input_border(0, f))
-        mid_one(p, 0, 2)
-        mid_one(p, rows, rows + 2)
-        outside(p, (act1, sl1))
+            border_arrived(input_border(which, f))
 
     w_copies[0].wait()
     arrange(0)
-    clear_rows((x1,))
-    stage_one(1)
+    for f in (2, 3):
+        load(0, f).wait()
+    mid_one(1, 2, rows)
     w_copies[1].wait()
     arrange(1)
-    for i, (lo, hi) in enumerate(PIECES):
-        second(1, lo, hi)
+    second(1, 2, 6)
+    when_start(has_next, a_piece(0))
+    second(1, 6, rows - 2)
+    for f in (0, 1):
+        load(0, f).wait()
+    mid_one(0, 2, rows)
+    second(0, 2, rows - 2)
+    clear_rows((x1,))
+    input_arrived(0, 1)
+    edges(mid_one, 1, 2)
+    outside(1, (act1, sl1))
+    edges(second, 1)
+    for i in range(1, len(PIECES)):
         when_start(has_next, a_piece(i))
-    stage_one(0)
-    second(0, 0, rows)
-    clear_rows((xc, x3, x5))
+    input_arrived(0, 0)
+    edges(mid_one, 0, 2)
+    outside(0, (act1, sl1))
+    edges(second, 0)
     for i in (2, 3, 4):
         w_copies[i].wait()
     arrange_lags()
-    for lo, hi in PIECES[:2]:
-        mix(1, lo, hi)
+    edges(mix, 1)
     border_start(pair_border(x3, x3s, x3r, 1))
     mix(1, 2, rows - 2)
+
+    clear_rows((xc, x3, x5))
+    for f in (2, 3, 0, 1):
+        load(1, f).wait()
+        border_arrived(input_border(1, f))
     arrange(2)
     arrange_back(3)
-    for f in (2, 3):
-        load(1, f).wait()
-        border_arrived(input_border(1, f))
     mid_four(1, 2, rows)
-    border_arrived(pair_border(x3, x3s, x3r, 1))
-    mid_four(1, 0, 2)
-    mid_four(1, rows, rows + 2)
-    outside(1, (act4, bk4))
     arrange_back(2)
-    back_three(1, 0, rows)
+    back_three(1, 2, rows - 2)
+    back_cotangent(0, rows + 2)
     arrange(3)
-    decode(1, 0, rows)
+    decode(1, 2, rows - 2)
     arrange_back(1)
     arrange_back(0)
     clear_frames()
-    for f in (0, 1):
-        load(1, f).wait()
-        border_arrived(input_border(1, f))
-
-    for i in (0, 1):
+    border_arrived(pair_border(x3, x3s, x3r, 1))
+    edges(mid_four, 1, 2)
+    outside(1, (act4, bk4))
+    edges(back_three, 1)
+    edges(decode, 1)
+
+    for i in (0, 1, 2):
         when_recv(has_prev, a_piece(i))
         mix(0, *PIECES[i])
     border_start(pair_border(x3, x3s, x3r, 0))
-    when_recv(has_prev, a_piece(2))
-    mix(0, *PIECES[2])
-    border_arrived(pair_border(x3, x3s, x3r, 0))
-    mid_four(0, 0, 8)
-    outside_first(0, (act4, bk4))
-    back_three(0, *BACK_PIECES[0])
-    when_start(has_prev, b_piece(0))
     when_recv(has_prev, a_piece(3))
     mix(0, *PIECES[3])
-    mid_four(0, 8, rows + 2)
-    outside_last(0, (act4, bk4))
-    for i in (1, 2, 3):
+    mid_four(0, 2, 10)
+    border_arrived(pair_border(x3, x3s, x3r, 0))
+    mid_four(0, 0, 2)
+    outside_first(0, (act4, bk4))
+    for i in (0, 1):
         back_three(0, *BACK_PIECES[i])
         when_start(has_prev, b_piece(i))
-    unmix(0, 0, 2)
-    unmix(0, rows - 2, rows)
+    when_recv(has_prev, a_piece(4))
+    mix(0, *PIECES[4])
+    mid_four(0, 10, rows + 2)
+    outside_last(0, (act4, bk4))
+    for i in (2, 3, 4):
+        back_three(0, *BACK_PIECES[i])
+        when_start(has_prev, b_piece(i))
+    edges(unmix, 0)
     border_start(pair_border(x5, x5s, x5r, 0))
     unmix(0, 2, rows - 2)
     decode(0, 0, rows)
+    back_one(0, 2, rows)
+    grads(2, rows - 2)
     border_arrived(pair_border(x5, x5s, x5r, 0))
-    back_one(0, 0, rows + 2)
-    grads(0, rows)
-
-    for i in (0, 1):
+    edges(back_one, 0, 2)
+    grads(0, 2)
+    grads(rows - 2, rows)
+
+    for i in (0, 1, 2):
         when_recv(has_next, b_piece(i))
         unmix(1, *BACK_PIECES[i])
     border_start(pair_border(x5, x5s, x5r, 1))
-    when_recv(has_next, b_piece(2))
-    unmix(1, *BACK_PIECES[2])
-    border_arrived(pair_border(x5, x5s, x5r, 1))
-    back_one(1, 0, 10)
     when_recv(has_next, b_piece(3))
     unmix(1, *BACK_PIECES[3])
-    back_one(1, 10, rows + 2)
+    back_one(1, 2, 11)
+    when_recv(has_next, b_piece(4))
+    unmix(1, *BACK_PIECES[4])
+    back_one(1, 11, rows)
+    border_arrived(pair_border(x5, x5s, x5r, 1))
+    edges(back_one, 1, 2)
 
     for which in range(2):
         for f in range(4):
@@ -436,7 +458,7 @@
             pair(4), pair(4), pair(4), pair(4),
             pair(2), pair(2),
             pair(0, count=3), pair(0), pair(0),
-            pair(2), pair(2),
+            pair(2), pair(2), pltpu.VMEM((rows + 2, C, 2 * W), f32),
             pair(0, count=3),
             pltpu.VMEM((rows + 2, C, 2 * W), bf16),
             pltpu.VMEM((4, *matrix), bf16), pltpu.VMEM((3, *matrix), bf16),
@@ -445,7 +467,7 @@
             dma((5,)), dma((2, 4)),
             dma((2, 4, 2)), dma((2, 4, 2)),
             dma((2, 2)), dma((2, 2)), dma((2, 2)), dma((2, 2)),
-            dma((4,)), dma((4,)), dma((4,)), dma((4,)),
+            dma((5,)), dma((5,)), dma((5,)), dma((5,)),
         ],
         compiler_params=pltpu.CompilerParams(collective_id=0, has_side_effects=True, vmem_limit_bytes=36 << 20),
     )(*[pltpu.with_memory_space_constraint(v, pltpu.HBM) for v in (frames_in, taps[0], taps[1], temporal, taps[2], taps[3], cotangent)])

time: 45.8 us -> 50.3 us (1.098)
  the two profiles are of different devices: /device:TPU:10 before, /device:TPU:1 now
where the time goes in v2:
time: 50.3 us; the launch traced here: 50.2 us
  Pallas kernels  49.4 us (98%)
  between operations  0.8 us (2%)
    pallas_call x1, Pallas kernels, per_device(): pl.pallas_call(functools.partial(kernel, sizes), name='stack', out_shape=...  47.2 us
    pallas_call x1, Pallas kernels, per_device(): pl.pallas_call(functools.partial(last_kernel, rows), name='last', out_sha...  2.2 us

profile of v2, /device:TPU:1, one launch (start us, length us, event | category | flops | bytes accessed | tf_op | source)
XLA Modules:
  0.0 50.2 jit_solution(10861842279131107261)
XLA Ops:
  0.6 47.2 %stack.1 = (bf16[2,16,64,256]{3,2,1,0:T(8,128)(2,1)S(1)}, f32[16,64,256]{2,1,0:T(8,128)S(1)}, bf16[18,64,256]{2,1,0:T(8,128)(2,1)S(1)}, bf16[192,192]{1,0:T(8,128)(2,1)S(1)}) custom-call(bf16[4,16,64,128]{3,2,1,0:T(8,128)(2,1)} %x_hbm.1, bf16[3,3,64,64]{3,2,1,0:T(8,128)(2,1)} %bitcast.4, bf16[3,3,64,64]{3,2,1,0:T(8,128)(2,1)} %bitcast.5, ...), custom_call_target="tpu_custom_call" | custom-call | tf_op jit(solution)/shard_map/stack/pallas_call | solution.py:446
  47.9 2.2 %last.1 = (bf16[4,16,64,128]{3,2,1,0:T(8,128)(2,1)}, f32[4,16,64,128]{3,2,1,0:T(8,128)}) custom-call(bf16[2,16,64,256]{3,2,1,0:T(8,128)(2,1)S(1)} %get-tuple-element.6.dec, f32[16,64,256]{2,1,0:T(8,128)S(1)} %get-tuple-element.7.grad0, bf16[18,64,256]{2,1,0:T(8,128)(2,1)S(1)} %get-tuple-element.8.bk1, bf16[192,192]{1,0:T(8,128)(2,1)S(1)} %get-tuple-element.9.bw1), custom_call_target="tpu_custom_call" | custom-call | tf_op jit(solution)/shard_map/last/pallas_call | solution.py:474

commit v3 on v2

--- a/solution.py
+++ b/solution.py
@@ -146,8 +146,8 @@
     def pair_border(buf, send, recv, p):
         return border(lambda r: buf.at[p, r + 2:r + 4], lambda r: buf.at[p, r:r + 2], send, recv, (p,))
 
-    for which, f in ((0, 2), (0, 3), (0, 0), (0, 1), (1, 2), (1, 3), (1, 0), (1, 1)):
-        border_start(input_border(which, f))
+    for f in (2, 3, 0, 1):
+        border_start(input_border(0, f))
 
     def a_piece(i):
         lo, hi = PIECES[i]
@@ -342,7 +342,11 @@
     edges(mid_one, 1, 2)
     outside(1, (act1, sl1))
     edges(second, 1)
-    for i in range(1, len(PIECES)):
+    for i in (1, 2):
+        when_start(has_next, a_piece(i))
+    for f in (2, 3, 0, 1):
+        border_start(input_border(1, f))
+    for i in (3, 4):
         when_start(has_next, a_piece(i))
     input_arrived(0, 0)
     edges(mid_one, 0, 2)
@@ -361,25 +365,25 @@
         border_arrived(input_border(1, f))
     arrange(2)
     arrange_back(3)
+    back_cotangent(0, rows + 2)
     mid_four(1, 2, rows)
+    clear_frames()
+    for i in (1, 2):
+        when_recv(has_prev, a_piece(i))
+        mix(0, *PIECES[i])
+    border_start(pair_border(x3, x3s, x3r, 0))
     arrange_back(2)
     back_three(1, 2, rows - 2)
-    back_cotangent(0, rows + 2)
-    arrange(3)
-    decode(1, 2, rows - 2)
-    arrange_back(1)
-    arrange_back(0)
-    clear_frames()
     border_arrived(pair_border(x3, x3s, x3r, 1))
     edges(mid_four, 1, 2)
     outside(1, (act4, bk4))
     edges(back_three, 1)
-    edges(decode, 1)
-
-    for i in (0, 1, 2):
-        when_recv(has_prev, a_piece(i))
-        mix(0, *PIECES[i])
-    border_start(pair_border(x3, x3s, x3r, 0))
+    arrange(3)
+    decode(1, 0, rows)
+    arrange_back(1)
+    arrange_back(0)
+    when_recv(has_prev, a_piece(0))
+    mix(0, *PIECES[0])
     when_recv(has_prev, a_piece(3))
     mix(0, *PIECES[3])
     mid_four(0, 2, 10)

time: 50.3 us -> 42.7 us (0.85)
  the two profiles are of different devices: /device:TPU:1 before, /device:TPU:14 now
where the time goes in v3:
time: 42.7 us; the launch traced here: 42.6 us
  Pallas kernels  41.8 us (98%)
  between operations  0.8 us (2%)
    pallas_call x1, Pallas kernels, per_device(): pl.pallas_call(functools.partial(kernel, sizes), name='stack', out_shape=...  39.6 us
    pallas_call x1, Pallas kernels, per_device(): pl.pallas_call(functools.partial(last_kernel, rows), name='last', out_sha...  2.2 us

profile of v3, /device:TPU:14, one launch (start us, length us, event | category | flops | bytes accessed | tf_op | source)
XLA Modules:
  0.0 42.6 jit_solution(17268504613538217780)
XLA Ops:
  0.6 39.6 %stack.1 = (bf16[2,16,64,256]{3,2,1,0:T(8,128)(2,1)S(1)}, f32[16,64,256]{2,1,0:T(8,128)S(1)}, bf16[18,64,256]{2,1,0:T(8,128)(2,1)S(1)}, bf16[192,192]{1,0:T(8,128)(2,1)S(1)}) custom-call(bf16[4,16,64,128]{3,2,1,0:T(8,128)(2,1)} %x_hbm.1, bf16[3,3,64,64]{3,2,1,0:T(8,128)(2,1)} %bitcast.4, bf16[3,3,64,64]{3,2,1,0:T(8,128)(2,1)} %bitcast.5, ...), custom_call_target="tpu_custom_call" | custom-call | tf_op jit(solution)/shard_map/stack/pallas_call | solution.py:450
  40.3 2.2 %last.1 = (bf16[4,16,64,128]{3,2,1,0:T(8,128)(2,1)}, f32[4,16,64,128]{3,2,1,0:T(8,128)}) custom-call(bf16[2,16,64,256]{3,2,1,0:T(8,128)(2,1)S(1)} %get-tuple-element.6.dec, f32[16,64,256]{2,1,0:T(8,128)S(1)} %get-tuple-element.7.grad0, bf16[18,64,256]{2,1,0:T(8,128)(2,1)S(1)} %get-tuple-element.8.bk1, bf16[192,192]{1,0:T(8,128)(2,1)S(1)} %get-tuple-element.9.bw1), custom_call_target="tpu_custom_call" | custom-call | tf_op jit(solution)/shard_map/last/pallas_call | solution.py:478

commit v4 on v3

--- a/solution.py
+++ b/solution.py
@@ -362,10 +362,9 @@
     clear_rows((xc, x3, x5))
     for f in (2, 3, 0, 1):
         load(1, f).wait()
-        border_arrived(input_border(1, f))
     arrange(2)
     arrange_back(3)
-    back_cotangent(0, rows + 2)
+    back_cotangent(2, rows)
     mid_four(1, 2, rows)
     clear_frames()
     for i in (1, 2):
@@ -374,14 +373,9 @@
     border_start(pair_border(x3, x3s, x3r, 0))
     arrange_back(2)
     back_three(1, 2, rows - 2)
-    border_arrived(pair_border(x3, x3s, x3r, 1))
-    edges(mid_four, 1, 2)
-    outside(1, (act4, bk4))
-    edges(back_three, 1)
-    arrange(3)
-    decode(1, 0, rows)
-    arrange_back(1)
-    arrange_back(0)
+    input_arrived(1, 0)
+    back_cotangent(0, 2)
+    back_cotangent(rows, rows + 2)
     when_recv(has_prev, a_piece(0))
     mix(0, *PIECES[0])
     when_recv(has_prev, a_piece(3))
@@ -392,17 +386,27 @@
     outside_first(0, (act4, bk4))
     for i in (0, 1):
         back_three(0, *BACK_PIECES[i])
+    when_recv(has_prev, a_piece(4))
+    for i in (0, 1):
         when_start(has_prev, b_piece(i))
-    when_recv(has_prev, a_piece(4))
     mix(0, *PIECES[4])
     mid_four(0, 10, rows + 2)
     outside_last(0, (act4, bk4))
     for i in (2, 3, 4):
         back_three(0, *BACK_PIECES[i])
         when_start(has_prev, b_piece(i))
+    input_arrived(1, 1)
+    border_arrived(pair_border(x3, x3s, x3r, 1))
+    edges(mid_four, 1, 2)
+    outside(1, (act4, bk4))
+    edges(back_three, 1)
     edges(unmix, 0)
     border_start(pair_border(x5, x5s, x5r, 0))
     unmix(0, 2, rows - 2)
+    arrange_back(1)
+    arrange_back(0)
+    arrange(3)
+    decode(1, 0, rows)
     decode(0, 0, rows)
     back_one(0, 2, rows)
     grads(2, rows - 2)

time: 42.7 us -> 44.3 us (1.037)
  the two profiles are of different devices: /device:TPU:14 before, /device:TPU:1 now
where the time goes in v4:
time: 44.3 us; the launch traced here: 44.2 us
  Pallas kernels  43.4 us (98%)
  between operations  0.8 us (2%)
    pallas_call x1, Pallas kernels, per_device(): pl.pallas_call(functools.partial(kernel, sizes), name='stack', out_shape=...  41.2 us
    pallas_call x1, Pallas kernels, per_device(): pl.pallas_call(functools.partial(last_kernel, rows), name='last', out_sha...  2.2 us

profile of v4, /device:TPU:1, one launch (start us, length us, event | category | flops | bytes accessed | tf_op | source)
XLA Modules:
  0.0 44.2 jit_solution(10163329644816036625)
XLA Ops:
  0.6 41.2 %stack.1 = (bf16[2,16,64,256]{3,2,1,0:T(8,128)(2,1)S(1)}, f32[16,64,256]{2,1,0:T(8,128)S(1)}, bf16[18,64,256]{2,1,0:T(8,128)(2,1)S(1)}, bf16[192,192]{1,0:T(8,128)(2,1)S(1)}) custom-call(bf16[4,16,64,128]{3,2,1,0:T(8,128)(2,1)} %x_hbm.1, bf16[3,3,64,64]{3,2,1,0:T(8,128)(2,1)} %bitcast.4, bf16[3,3,64,64]{3,2,1,0:T(8,128)(2,1)} %bitcast.5, ...), custom_call_target="tpu_custom_call" | custom-call | tf_op jit(solution)/shard_map/stack/pallas_call | solution.py:454
  41.9 2.2 %last.1 = (bf16[4,16,64,128]{3,2,1,0:T(8,128)(2,1)}, f32[4,16,64,128]{3,2,1,0:T(8,128)}) custom-call(bf16[2,16,64,256]{3,2,1,0:T(8,128)(2,1)S(1)} %get-tuple-element.6.dec, f32[16,64,256]{2,1,0:T(8,128)S(1)} %get-tuple-element.7.grad0, bf16[18,64,256]{2,1,0:T(8,128)(2,1)S(1)} %get-tuple-element.8.bk1, bf16[192,192]{1,0:T(8,128)(2,1)S(1)} %get-tuple-element.9.bw1), custom_call_target="tpu_custom_call" | custom-call | tf_op jit(solution)/shard_map/last/pallas_call | solution.py:482
